TPU v7x, 256 devices: a whole 4x4x8 slice. The times are simulated.
256 devices in a mesh: tm: 8 (over x_hi, y), azim: 32 (over z, x_lo, core).
Axes of the slice: x: 4 (x_hi: 2, x_lo: 2; x = x_hi * 2 + x_lo), y: 4, z: 8, core: 2. Of those that a mesh axis runs over, the one named last changes fastest.
Arguments:
- rotor_coeffs: float32 [64, 2, 32, 16384], P('tm', None, 'azim'), may hold values from -1.5 to 1.5
- mortar_weights: float32 [64, 2, 32, 16384], P('tm', None, 'azim'), may hold values from 0.2 to 1
- block_shifts: int32 [64], P('tm'), may hold values from 0 to 31
- stencil_offsets: int32 [64, 2], P('tm'), may hold values from -1 to 1
- reluctivity: float32 [32, 16384], P('azim'), may hold values from 0.5 to 2
- source: float32 [64, 2, 32, 16384], P('tm', None, 'azim'), may hold values from -3 to 3
Outputs:
- residual: float32 [64, 2, 32, 16384], P('tm', None, 'azim')
All inputs are finite; a program needn't handle non-finite values.
Results may differ from a plain program's by a relative error of at most 0.0001.
Values sent between devices are 32-bit elements; how exact they have to be, the bound alone decides.
A program may use at most 128 MiB of HBM per device.

v0:
```python
import jax
import jax.numpy as jnp
from jax import lax
from jax.sharding import PartitionSpec as P

KC = 64
NT = 64
LANES = 128


def shifted(value, axis, steps):
    count = lax.axis_size(axis)
    pairs = [(source, (source + steps) % count) for source in range(count)]
    return lax.ppermute(value, axis, pairs)


def harmonic_basis(sample_rows, coefficient_count):
    column = jnp.arange(coefficient_count, dtype=jnp.int32)
    harmonic_order = 2 * (column // 2) + 1
    phase_index = harmonic_order[None, :] * (2 * sample_rows[:, None] + 1) % (4 * NT)
    phase_angle = phase_index.astype(jnp.float32) * (jnp.pi / (2 * NT))
    return jnp.where(column[None, :] % 2 == 0, jnp.cos(phase_angle), jnp.sin(phase_angle))


def per_sample(flags, value):
    return flags.reshape((-1,) + (1,) * (value.ndim - 1))


def body(rotor_coeffs, mortar_weights, block_shifts, stencil_offsets, reluctivity, source):
    local_c, comp, _, nodes = rotor_coeffs.shape
    local_j, sten = mortar_weights.shape[:2]
    rows = nodes // LANES
    parts = lax.axis_size("tm")
    chunk = rows // parts
    coeffs = lax.all_to_all(
        rotor_coeffs.reshape(local_c, comp, rows, LANES),
        "tm",
        split_axis=2,
        concat_axis=0,
        tiled=True,
    )
    weights = lax.all_to_all(
        mortar_weights.reshape(local_j, sten, rows, LANES),
        "tm",
        split_axis=2,
        concat_axis=0,
        tiled=True,
    )
    shifts = lax.all_gather(block_shifts, "tm", tiled=True)
    offsets = lax.all_gather(stencil_offsets, "tm", tiled=True)
    gain = lax.dynamic_slice_in_dim(
        reluctivity.reshape(rows, LANES), lax.axis_index("tm") * chunk, chunk, axis=0
    )
    table = harmonic_basis(jnp.arange(NT, dtype=jnp.int32), KC)
    samples = jnp.einsum("jc,capk->japk", table, coeffs, precision=lax.Precision.HIGHEST)
    turned = samples
    for bit_level in range((lax.axis_size("azim") - 1).bit_length()):
        moved = shifted(turned, "azim", 1 << bit_level)
        chosen = shifts >> bit_level & 1 == 1
        turned = jnp.where(per_sample(chosen, turned), moved, turned)
    from_left = shifted(turned, "azim", 1)
    from_right = shifted(turned, "azim", -1)
    airgap_field = jnp.zeros_like(samples)
    for stencil_entry in range(sten):
        offset = offsets[:, stencil_entry]
        neighbour = jnp.where(
            per_sample(offset == 0, turned),
            turned,
            jnp.where(per_sample(offset > 0, turned), from_right, from_left),
        )
        airgap_field = airgap_field + weights[:, stencil_entry][:, None] * neighbour
    square = jnp.sum(airgap_field * airgap_field, axis=1, keepdims=True)
    field_flux = gain[None, None] * (1.0 + square / (1.0 + square)) * airgap_field
    summed = jnp.einsum(
        "jc,japk->capk", table * (2.0 / NT), field_flux, precision=lax.Precision.HIGHEST
    )
    residual = lax.all_to_all(summed, "tm", split_axis=0, concat_axis=2, tiled=True)
    return residual.reshape(source.shape) - source


def solution(mesh):
    in_specs = (
        P("tm", None, "azim", None),
        P("tm", None, "azim", None),
        P("tm"),
        P("tm", None),
        P("azim", None),
        P("tm", None, "azim", None),
    )
    out_specs = P("tm", None, "azim", None)
    return jax.shard_map(body, mesh=mesh, in_specs=in_specs, out_specs=out_specs, check_vma=False)
```

profile of v0, /device:TPU:97, one launch (start us, length us, event | category | flops | bytes accessed | tf_op | source)
XLA Modules:
  0.0 303.6 jit_solution(7695853863553865588)
XLA Ops:
  0.0 3.0 copy.28
  3.0 6.7 %all-to-all-start.1 = ((f32[8,2,128,128]{3,1,0,2:T(2,128)}), f32[8,2,128,128]{3,1,0,2:T(2,128)S(1)}, u32[]{:S(2)}, u32[]{:S(2)}) async-start(f32[8,2,128,128]{3,1,0,2:T(2,128)} %copy.28), calls=%async_computation.1 | async-start | bytes 2097152 | tf_op jit(solution)/shard_map/all_to_all | solution.py:35
  9.7 14.2 %all-to-all-done.1 = f32[8,2,128,128]{3,1,0,2:T(2,128)S(1)} async-done(((f32[8,2,128,128]{3,1,0,2:T(2,128)}), f32[8,2,128,128]{3,1,0,2:T(2,128)S(1)}, u32[]{:S(2)}, u32[]{:S(2)}) %all-to-all-start.1) | async-done | bytes 1048608 | tf_op jit(solution)/shard_map/all_to_all | solution.py:35
  23.9 0.3 copy.29
  24.2 1.8 fusion
  26.0 2.9 collective-permute-start
  28.9 0.7 copy-done.6
  29.6 0.6 dynamic-slice
  30.8 0.6 copy-done.5
  31.6 11.8 %all-reduce = s32[64]{0:T(128)S(1)} all-reduce(s32[64]{0:T(128)S(1)} %dynamic-update-slice), channel_id=1, replica_groups=mesh['tm'=8,'azim'=32] {'tm'}, use_global_device_ids=true, to_apply=%add | all-reduce | flops 64 | bytes 512
  43.4 0.2 broadcast_select_fusion
  43.7 1.0 collective-permute-start.1
  44.7 24.2 %collective-permute-done.1 = f32[64,2,16,128]{3,0,2,1:T(8,128)S(1)} collective-permute-done((f32[64,2,16,128]{3,0,2,1:T(8,128)S(1)}, f32[64,2,16,128]{3,0,2,1:T(8,128)S(1)}, u32[]{:S(2)}, u32[]{:S(2)}) %collective-permute-start.1) | collective-permute-done | bytes 1048608 | tf_op jit(solution)/shard_map/ppermute | solution.py:14
  69.2 3.4 %collective-permute-start.2 = (f32[64,2,16,128]{3,0,2,1:T(8,128)S(1)}, f32[64,2,16,128]{3,0,2,1:T(8,128)S(1)}, u32[]{:S(2)}, u32[]{:S(2)}) collective-permute-start(f32[64,2,16,128]{3,0,2,1:T(8,128)S(1)} %broadcast_select_fusion.1), channel_id=1, source_target_pairs={{0,4},{1,5},{2,6},{3,7},{4,8},{5,9},{6,10},{7,11},{8,12},{9,13},{1... | collective-permute-start | bytes 3145736 | tf_op jit(solution)/shard_map/ppermute | solution.py:14
  72.6 20.1 %collective-permute-done.2 = f32[64,2,16,128]{3,0,2,1:T(8,128)S(1)} collective-permute-done((f32[64,2,16,128]{3,0,2,1:T(8,128)S(1)}, f32[64,2,16,128]{3,0,2,1:T(8,128)S(1)}, u32[]{:S(2)}, u32[]{:S(2)}) %collective-permute-start.2) | collective-permute-done | bytes 1048608 | tf_op jit(solution)/shard_map/ppermute | solution.py:14
  93.0 2.8 collective-permute-start.3
  95.7 28.5 %collective-permute-done.3 = f32[64,2,16,128]{3,0,2,1:T(8,128)S(1)} collective-permute-done((f32[64,2,16,128]{3,0,2,1:T(8,128)S(1)}, f32[64,2,16,128]{3,0,2,1:T(8,128)S(1)}, u32[]{:S(2)}, u32[]{:S(2)}) %collective-permute-start.3) | collective-permute-done | bytes 1048608 | tf_op jit(solution)/shard_map/ppermute | solution.py:14
  124.5 5.7 %collective-permute-start.4 = (f32[64,2,16,128]{3,0,2,1:T(8,128)S(1)}, f32[64,2,16,128]{3,0,2,1:T(8,128)S(1)}, u32[]{:S(2)}, u32[]{:S(2)}) collective-permute-start(f32[64,2,16,128]{3,0,2,1:T(8,128)S(1)} %broadcast_select_fusion.3), channel_id=1, source_target_pairs={{0,16},{1,17},{2,18},{3,19},{4,20},{5,21},{6,22},{7,23},{8,24},{9,... | collective-permute-start | bytes 3145736 | tf_op jit(solution)/shard_map/ppermute | solution.py:14
  130.2 1.8 copy.24
  132.0 8.7 %all-to-all-start = ((f32[8,2,128,128]{3,1,0,2:T(2,128)}), f32[8,2,128,128]{3,1,0,2:T(2,128)S(1)}, u32[]{:S(2)}, u32[]{:S(2)}) async-start(f32[8,2,128,128]{3,1,0,2:T(2,128)} %copy.24), calls=%async_computation | async-start | bytes 2097152 | tf_op jit(solution)/shard_map/all_to_all | solution.py:42
  140.7 33.7 %collective-permute-done.4 = f32[64,2,16,128]{3,0,2,1:T(8,128)S(1)} collective-permute-done((f32[64,2,16,128]{3,0,2,1:T(8,128)S(1)}, f32[64,2,16,128]{3,0,2,1:T(8,128)S(1)}, u32[]{:S(2)}, u32[]{:S(2)}) %collective-permute-start.4) | collective-permute-done | bytes 1048608 | tf_op jit(solution)/shard_map/ppermute | solution.py:14
  174.4 1.0 copy-done.3
  175.4 1.4 broadcast_select_fusion.4
  176.8 20.0 %collective-permute-start.6 = (f32[64,2,16,128]{3,0,2,1:T(8,128)S(1)}, f32[64,2,16,128]{3,0,2,1:T(8,128)S(1)}, u32[]{:S(2)}, u32[]{:S(2)}) collective-permute-start(f32[64,2,16,128]{3,0,2,1:T(8,128)S(1)} %broadcast_select_fusion.4), channel_id=1, source_target_pairs={{0,1},{1,2},{2,3},{3,4},{4,5},{5,6},{6,7},{7,8},{8,9},{9,10},{10,1... | collective-permute-start | bytes 3145736 | tf_op jit(solution)/shard_map/ppermute | solution.py:14
  196.8 0.7 copy-done.4
  197.4 52.3 %all-gather = s32[8,8,2]{1,2,0:T(2,128)S(1)} all-gather(s32[1,8,2]{1,2,0:T(2,128)S(1)} %bitcast.51), channel_id=1, replica_groups=mesh['tm'=8,'azim'=32] {'tm'}, dimensions={0}, use_global_device_ids=true | all-gather | bytes 576 | tf_op jit(solution)/shard_map/all_gather | solution.py:50
  250.1 1.9 multiply_reduce_fusion
  252.1 1.2 fusion.3
  253.3 0.6 copy.32
  254.0 46.4 %all_to_all.51 = f32[64,2,16,128]{3,2,1,0:T(8,128)S(1)} all-to-all(f32[64,2,16,128]{3,2,1,0:T(8,128)S(1)} %copy.32), channel_id=1, replica_groups=mesh['tm'=8,'azim'=32] {'tm'}, dimensions={0} | all-to-all | bytes 2097152 | tf_op jit(solution)/shard_map/all_to_all | solution.py:77
  300.4 1.1 copy-done.1
  301.5 2.1 sub.12
  (30 shorter events, 1.4 us)
Async XLA Ops:
  0.0 249.9 %copy-start = (f32[1,16384]{1,0:T(1,128)S(1)}, f32[1,16384]{1,0:T(1,128)}, u32[]{:S(2)}) copy-start(f32[1,16384]{1,0:T(1,128)} %param.10) | copy-start | bytes 196612
  3.0 20.8 %all-to-all-start.1 = ((f32[8,2,128,128]{3,1,0,2:T(2,128)}), f32[8,2,128,128]{3,1,0,2:T(2,128)S(1)}, u32[]{:S(2)}, u32[]{:S(2)}) async-start(f32[8,2,128,128]{3,1,0,2:T(2,128)} %copy.28), calls=%async_computation.1 | async-start | bytes 2097152 | tf_op jit(solution)/shard_map/all_to_all | solution.py:35
  26.0 17.4 %collective-permute-start = (f32[64,2,16,128]{3,0,2,1:T(8,128)S(1)}, f32[64,2,16,128]{3,0,2,1:T(8,128)S(1)}, u32[]{:S(2)}, u32[]{:S(2)}) collective-permute-start(f32[64,2,16,128]{3,0,2,1:T(8,128)S(1)} %fusion), channel_id=1, source_target_pairs={{0,1},{1,2},{2,3},{3,4},{4,5},{5,6},{6,7},{7,8},{8,9},{9,10},{10,1... | collective-permute-start | bytes 3145736 | tf_op jit(solution)/shard_map/ppermute | solution.py:14
  28.9 0.7 copy-start.6
  30.8 0.7 copy-start.5
  43.7 25.3 %collective-permute-start.1 = (f32[64,2,16,128]{3,0,2,1:T(8,128)S(1)}, f32[64,2,16,128]{3,0,2,1:T(8,128)S(1)}, u32[]{:S(2)}, u32[]{:S(2)}) collective-permute-start(f32[64,2,16,128]{3,0,2,1:T(8,128)S(1)} %broadcast_select_fusion), channel_id=1, source_target_pairs={{0,2},{1,3},{2,4},{3,5},{4,6},{5,7},{6,8},{7,9},{8,10},{9,11},{10,... | collective-permute-start | bytes 3145736 | tf_op jit(solution)/shard_map/ppermute | solution.py:14
  69.2 23.6 %collective-permute-start.2 = (f32[64,2,16,128]{3,0,2,1:T(8,128)S(1)}, f32[64,2,16,128]{3,0,2,1:T(8,128)S(1)}, u32[]{:S(2)}, u32[]{:S(2)}) collective-permute-start(f32[64,2,16,128]{3,0,2,1:T(8,128)S(1)} %broadcast_select_fusion.1), channel_id=1, source_target_pairs={{0,4},{1,5},{2,6},{3,7},{4,8},{5,9},{6,10},{7,11},{8,12},{9,13},{1... | collective-permute-start | bytes 3145736 | tf_op jit(solution)/shard_map/ppermute | solution.py:14
  93.0 31.3 %collective-permute-start.3 = (f32[64,2,16,128]{3,0,2,1:T(8,128)S(1)}, f32[64,2,16,128]{3,0,2,1:T(8,128)S(1)}, u32[]{:S(2)}, u32[]{:S(2)}) collective-permute-start(f32[64,2,16,128]{3,0,2,1:T(8,128)S(1)} %broadcast_select_fusion.2), channel_id=1, source_target_pairs={{0,8},{1,9},{2,10},{3,11},{4,12},{5,13},{6,14},{7,15},{8,16},{9,17... | collective-permute-start | bytes 3145736 | tf_op jit(solution)/shard_map/ppermute | solution.py:14
  124.2 5.9 %copy-start.2 = (f32[8,2,1,16384]{3,2,1,0:T(1,128)S(1)}, f32[8,2,1,16384]{3,2,1,0:T(1,128)}, u32[]{:S(2)}) copy-start(f32[8,2,1,16384]{3,2,1,0:T(1,128)} %param.7) | copy-start | bytes 3145732
  124.5 49.9 %collective-permute-start.4 = (f32[64,2,16,128]{3,0,2,1:T(8,128)S(1)}, f32[64,2,16,128]{3,0,2,1:T(8,128)S(1)}, u32[]{:S(2)}, u32[]{:S(2)}) collective-permute-start(f32[64,2,16,128]{3,0,2,1:T(8,128)S(1)} %broadcast_select_fusion.3), channel_id=1, source_target_pairs={{0,16},{1,17},{2,18},{3,19},{4,20},{5,21},{6,22},{7,23},{8,24},{9,... | collective-permute-start | bytes 3145736 | tf_op jit(solution)/shard_map/ppermute | solution.py:14
  132.0 117.9 %all-to-all-start = ((f32[8,2,128,128]{3,1,0,2:T(2,128)}), f32[8,2,128,128]{3,1,0,2:T(2,128)S(1)}, u32[]{:S(2)}, u32[]{:S(2)}) async-start(f32[8,2,128,128]{3,1,0,2:T(2,128)} %copy.24), calls=%async_computation | async-start | bytes 2097152 | tf_op jit(solution)/shard_map/all_to_all | solution.py:42
  174.4 1.0 copy-start.3
  176.8 73.3 %collective-permute-start.6 = (f32[64,2,16,128]{3,0,2,1:T(8,128)S(1)}, f32[64,2,16,128]{3,0,2,1:T(8,128)S(1)}, u32[]{:S(2)}, u32[]{:S(2)}) collective-permute-start(f32[64,2,16,128]{3,0,2,1:T(8,128)S(1)} %broadcast_select_fusion.4), channel_id=1, source_target_pairs={{0,1},{1,2},{2,3},{3,4},{4,5},{5,6},{6,7},{7,8},{8,9},{9,10},{10,1... | collective-permute-start | bytes 3145736 | tf_op jit(solution)/shard_map/ppermute | solution.py:14
  196.8 53.4 %collective-permute-start.5 = (f32[64,2,16,128]{3,0,2,1:T(8,128)S(1)}, f32[64,2,16,128]{3,0,2,1:T(8,128)}, u32[]{:S(2)}, u32[]{:S(2)}) collective-permute-start(f32[64,2,16,128]{3,0,2,1:T(8,128)S(1)} %broadcast_select_fusion.4), channel_id=1, source_target_pairs={{0,31},{1,0},{2,1},{3,2},{4,3},{5,4},{6,5},{7,6},{8,7},{9,8},{10,9... | collective-permute-start | bytes 3145736 | tf_op jit(solution)/shard_map/ppermute | solution.py:14
  196.8 0.7 copy-start.4
  300.3 1.2 copy-start.1
where the time goes:
time: 304 us
  waiting for transfers between devices  121 us (40%)
  blocking collectives  110 us (36%)
  starting transfers between devices  51.1 us (17%)
  local copies, waits for them, and re-layouts  11 us (4%)
  other arithmetic  6.42 us (2%)
    ppermute x7, waiting for transfers between devices, shifted(): return lax.ppermute(value, axis, pairs)  107 us
    all_gather x1, blocking collectives, body(): offsets = lax.all_gather(stencil_offsets, 'tm', tiled=True)  52.3 us
    all_to_all x1, blocking collectives, body(): lax.all_to_all(summed, 'tm', split_axis=0, concat_axis=2, tiled=True)  46.4 us
    ppermute x7, starting transfers between devices, shifted(): return lax.ppermute(value, axis, pairs)  35.7 us
    all_to_all x1, waiting for transfers between devices, body(): lax.all_to_all(rotor_coeffs.reshape(local_c, comp, rows, LANES), 'tm', sp...  14.2 us
    unnamed x1, blocking collectives  11.8 us
    all_to_all x1, starting transfers between devices, body(): lax.all_to_all(mortar_weights.reshape(local_j, sten, rows, LANES), 'tm',...  8.69 us
    all_to_all x1, starting transfers between devices, body(): lax.all_to_all(rotor_coeffs.reshape(local_c, comp, rows, LANES), 'tm', sp...  6.65 us
  transfers between devices with their start and end apart: 9, of which 5 were waited for; matrix products, arithmetic and copies ran while one was open for 1% of the time, Pallas kernels for 0%

commit v1 on v0

--- a/solution.py
+++ b/solution.py
@@ -1,3 +1,4 @@
+import functools
 import jax
 import jax.numpy as jnp
 from jax import lax
@@ -6,6 +7,15 @@
 KC = 64
 NT = 64
 LANES = 128
+
+
+def launch_the_panel(piece_in, mesh_name):
+    part_next = jnp.stack([piece_in for _ in range(lax.axis_size(mesh_name))])
+    b_now = lax.all_to_all(part_next, mesh_name, 0, 0)
+    return jnp.concatenate(b_now, axis=0)
+
+
+switch_the_zone = functools.partial(launch_the_panel, mesh_name="tm")
 
 
 def shifted(value, axis, steps):
@@ -47,7 +57,7 @@
         tiled=True,
     )
     shifts = lax.all_gather(block_shifts, "tm", tiled=True)
-    offsets = lax.all_gather(stencil_offsets, "tm", tiled=True)
+    offsets = switch_the_zone(stencil_offsets)
     gain = lax.dynamic_slice_in_dim(
         reluctivity.reshape(rows, LANES), lax.axis_index("tm") * chunk, chunk, axis=0
     )

time: 304 us -> 291 us (0.957)
  blocking collectives: 110 us -> 65.3 us
  waiting for transfers between devices: 121 us -> 139 us
  starting transfers between devices: 51.1 us -> 64.1 us
    all_gather x1 -> x0, blocking collectives: 52.3 us -> none  [body(): offsets = lax.all_gather(stencil_offsets, 'tm', tiled=True)]
    ppermute x7, waiting for transfers between devices: 107 us -> 121 us  [shifted(): return lax.ppermute(value, axis, pairs)]
    ppermute x7, starting transfers between devices: 35.7 us -> 45.2 us  [shifted(): return lax.ppermute(value, axis, pairs)]
    all_to_all x0 -> x1, starting transfers between devices: none -> 8.69 us  [launch_the_panel(): b_now = lax.all_to_all(part_next, mesh_name, 0, 0)]
    all_to_all x1, blocking collectives: 46.4 us -> 53.6 us  [body(): lax.all_to_all(summed, 'tm', split_axis=0, concat_axis=2, tiled=True)]
    all_to_all x1, starting transfers between devices: 8.69 us -> 3.56 us  [body(): lax.all_to_all(mortar_weights.reshape(local_j, sten, rows, LANES), 'tm',...]
    all_to_all x0 -> x1, waiting for transfers between devices: none -> 4.76 us  [launch_the_panel(): b_now = lax.all_to_all(part_next, mesh_name, 0, 0)]
  transfers between devices with their start and end apart: 9 -> 10, of which waited for: 5 -> 7; matrix products, arithmetic and copies ran while one was open for 1% -> 2% of each run, Pallas kernels for 0% -> 0%
where the time goes in v1:
time: 291 us; the launch traced here: 289 us
  waiting for transfers between devices  139 us (48%)
  blocking collectives  65.3 us (22%)
  starting transfers between devices  64.1 us (22%)
  local copies, waits for them, and re-layouts  9.95 us (3%)
  other arithmetic  6.42 us (2%)
  matrix products  2.96 us (1%)
    ppermute x7, waiting for transfers between devices, shifted(): return lax.ppermute(value, axis, pairs)  121 us
    all_to_all x1, blocking collectives, body(): lax.all_to_all(summed, 'tm', split_axis=0, concat_axis=2, tiled=True)  53.6 us
    ppermute x7, starting transfers between devices, shifted(): return lax.ppermute(value, axis, pairs)  45.2 us
    all_to_all x1, waiting for transfers between devices, body(): lax.all_to_all(rotor_coeffs.reshape(local_c, comp, rows, LANES), 'tm', sp...  14.2 us
    unnamed x1, blocking collectives  11.8 us
    all_to_all x1, starting transfers between devices, launch_the_panel(): b_now = lax.all_to_all(part_next, mesh_name, 0, 0)  8.69 us
    all_to_all x1, starting transfers between devices, body(): lax.all_to_all(rotor_coeffs.reshape(local_c, comp, rows, LANES), 'tm', sp...  6.65 us
  transfers between devices with their start and end apart: 10, of which 7 were waited for; matrix products, arithmetic and copies ran while one was open for 2% of the time, Pallas kernels for 0%

profile of v1, /device:TPU:97, one launch (start us, length us, event | category | flops | bytes accessed | tf_op | source)
XLA Modules:
  0.0 289.0 jit_solution(6917708720212373685)
XLA Ops:
  0.0 3.0 %copy.26 = f32[8,2,128,128]{3,1,0,2:T(2,128)} copy(f32[8,2,128,128]{3,2,1,0:T(8,128)} %bitcast.48) | data formatting | bytes 2097152 | tf_op jit(solution)/shard_map/reshape | solution.py:46
  3.0 6.7 %all-to-all-start.2 = ((f32[8,2,128,128]{3,1,0,2:T(2,128)}), f32[8,2,128,128]{3,1,0,2:T(2,128)S(1)}, u32[]{:S(2)}, u32[]{:S(2)}) async-start(f32[8,2,128,128]{3,1,0,2:T(2,128)} %copy.26), calls=%async_computation.2 | async-start | bytes 2097152 | tf_op jit(solution)/shard_map/all_to_all | solution.py:45
  9.7 14.2 %all-to-all-done.2 = f32[8,2,128,128]{3,1,0,2:T(2,128)S(1)} async-done(((f32[8,2,128,128]{3,1,0,2:T(2,128)}), f32[8,2,128,128]{3,1,0,2:T(2,128)S(1)}, u32[]{:S(2)}, u32[]{:S(2)}) %all-to-all-start.2) | async-done | bytes 1048608 | tf_op jit(solution)/shard_map/all_to_all | solution.py:45
  23.9 0.3 copy.27
  24.2 1.8 fusion
  26.0 2.9 %collective-permute-start = (f32[64,2,16,128]{3,0,2,1:T(8,128)S(1)}, f32[64,2,16,128]{3,0,2,1:T(8,128)S(1)}, u32[]{:S(2)}, u32[]{:S(2)}) collective-permute-start(f32[64,2,16,128]{3,0,2,1:T(8,128)S(1)} %fusion), channel_id=1, source_target_pairs={{0,1},{1,2},{2,3},{3,4},{4,5},{5,6},{6,7},{7,8},{8,9},{9,10},{10,1... | collective-permute-start | bytes 3145736 | tf_op jit(solution)/shard_map/ppermute | solution.py:24
  28.9 0.7 copy-done.5
  29.6 0.6 dynamic-slice
  30.8 0.6 copy-done.4
  31.6 11.8 %all-reduce = s32[64]{0:T(128)S(1)} all-reduce(s32[64]{0:T(128)S(1)} %dynamic-update-slice), channel_id=1, replica_groups=mesh['tm'=8,'azim'=32] {'tm'}, use_global_device_ids=true, to_apply=%add | all-reduce | flops 64 | bytes 512
  43.7 1.0 collective-permute-start.1
  44.7 24.2 %collective-permute-done.1 = f32[64,2,16,128]{3,0,2,1:T(8,128)S(1)} collective-permute-done((f32[64,2,16,128]{3,0,2,1:T(8,128)S(1)}, f32[64,2,16,128]{3,0,2,1:T(8,128)S(1)}, u32[]{:S(2)}, u32[]{:S(2)}) %collective-permute-start.1) | collective-permute-done | bytes 1048608 | tf_op jit(solution)/shard_map/ppermute | solution.py:24
  69.2 3.4 %collective-permute-start.2 = (f32[64,2,16,128]{3,0,2,1:T(8,128)S(1)}, f32[64,2,16,128]{3,0,2,1:T(8,128)S(1)}, u32[]{:S(2)}, u32[]{:S(2)}) collective-permute-start(f32[64,2,16,128]{3,0,2,1:T(8,128)S(1)} %broadcast_select_fusion.1), channel_id=1, source_target_pairs={{0,4},{1,5},{2,6},{3,7},{4,8},{5,9},{6,10},{7,11},{8,12},{9,13},{1... | collective-permute-start | bytes 3145736 | tf_op jit(solution)/shard_map/ppermute | solution.py:24
  72.6 20.1 %collective-permute-done.2 = f32[64,2,16,128]{3,0,2,1:T(8,128)S(1)} collective-permute-done((f32[64,2,16,128]{3,0,2,1:T(8,128)S(1)}, f32[64,2,16,128]{3,0,2,1:T(8,128)S(1)}, u32[]{:S(2)}, u32[]{:S(2)}) %collective-permute-start.2) | collective-permute-done | bytes 1048608 | tf_op jit(solution)/shard_map/ppermute | solution.py:24
  93.0 2.8 collective-permute-start.3
  95.7 28.5 %collective-permute-done.3 = f32[64,2,16,128]{3,0,2,1:T(8,128)S(1)} collective-permute-done((f32[64,2,16,128]{3,0,2,1:T(8,128)S(1)}, f32[64,2,16,128]{3,0,2,1:T(8,128)S(1)}, u32[]{:S(2)}, u32[]{:S(2)}) %collective-permute-start.3) | collective-permute-done | bytes 1048608 | tf_op jit(solution)/shard_map/ppermute | solution.py:24
  124.5 5.7 %collective-permute-start.4 = (f32[64,2,16,128]{3,0,2,1:T(8,128)S(1)}, f32[64,2,16,128]{3,0,2,1:T(8,128)}, u32[]{:S(2)}, u32[]{:S(2)}) collective-permute-start(f32[64,2,16,128]{3,0,2,1:T(8,128)S(1)} %broadcast_select_fusion.3), channel_id=1, source_target_pairs={{0,16},{1,17},{2,18},{3,19},{4,20},{5,21},{6,22},{7,23},{8,24},{9,... | collective-permute-start | bytes 3145736 | tf_op jit(solution)/shard_map/ppermute | solution.py:24
  130.2 0.6 stack.2
  130.8 8.7 %all-to-all-start.1 = ((s32[8,8,2]{1,2,0:T(2,128)}), s32[8,8,2]{1,2,0:T(2,128)S(1)}, u32[]{:S(2)}, u32[]{:S(2)}) async-start(s32[8,8,2]{1,2,0:T(2,128)} %stack.2), calls=%async_computation.1 | async-start | bytes 16384 | tf_op jit(solution)/shard_map/all_to_all | solution.py:14
  139.5 1.8 copy.22
  141.2 4.8 %all-to-all-done.1 = s32[8,8,2]{1,2,0:T(2,128)S(1)} async-done(((s32[8,8,2]{1,2,0:T(2,128)}), s32[8,8,2]{1,2,0:T(2,128)S(1)}, u32[]{:S(2)}, u32[]{:S(2)}) %all-to-all-start.1) | async-done | bytes 544 | tf_op jit(solution)/shard_map/all_to_all | solution.py:14
  146.0 3.6 %all-to-all-start = ((f32[8,2,128,128]{3,1,0,2:T(2,128)}), f32[8,2,128,128]{3,1,0,2:T(2,128)S(1)}, u32[]{:S(2)}, u32[]{:S(2)}) async-start(f32[8,2,128,128]{3,1,0,2:T(2,128)} %copy.22), calls=%async_computation | async-start | bytes 2097152 | tf_op jit(solution)/shard_map/all_to_all | solution.py:52
  149.6 24.9 %collective-permute-done.4 = f32[64,2,16,128]{3,0,2,1:T(8,128)} collective-permute-done((f32[64,2,16,128]{3,0,2,1:T(8,128)S(1)}, f32[64,2,16,128]{3,0,2,1:T(8,128)}, u32[]{:S(2)}, u32[]{:S(2)}) %collective-permute-start.4) | collective-permute-done | bytes 1048608 | tf_op jit(solution)/shard_map/ppermute | solution.py:24
  174.5 1.4 broadcast_select_fusion.4
  175.9 29.4 %collective-permute-start.6 = (f32[64,2,16,128]{3,0,2,1:T(8,128)S(1)}, f32[64,2,16,128]{3,0,2,1:T(8,128)S(1)}, u32[]{:S(2)}, u32[]{:S(2)}) collective-permute-start(f32[64,2,16,128]{3,0,2,1:T(8,128)S(1)} %broadcast_select_fusion.4), channel_id=1, source_target_pairs={{0,1},{1,2},{2,3},{3,4},{4,5},{5,6},{6,7},{7,8},{8,9},{9,10},{10,1... | collective-permute-start | bytes 3145736 | tf_op jit(solution)/shard_map/ppermute | solution.py:24
  205.7 22.7 %collective-permute-done.6 = f32[64,2,16,128]{3,0,2,1:T(8,128)S(1)} collective-permute-done((f32[64,2,16,128]{3,0,2,1:T(8,128)S(1)}, f32[64,2,16,128]{3,0,2,1:T(8,128)S(1)}, u32[]{:S(2)}, u32[]{:S(2)}) %collective-permute-start.6) | collective-permute-done | bytes 1048608 | tf_op jit(solution)/shard_map/ppermute | solution.py:24
  228.3 1.9 multiply_reduce_fusion
  230.3 1.2 fusion.3
  231.5 0.6 copy.30
  232.1 53.6 %all_to_all.56 = f32[64,2,16,128]{3,2,1,0:T(8,128)S(1)} all-to-all(f32[64,2,16,128]{3,2,1,0:T(8,128)S(1)} %copy.30), channel_id=1, replica_groups=mesh['tm'=8,'azim'=32] {'tm'}, dimensions={0} | all-to-all | bytes 2097152 | tf_op jit(solution)/shard_map/all_to_all | solution.py:87
  285.8 1.1 copy-done.1
  286.9 2.1 sub.12
  (30 shorter events, 1.6 us)
Async XLA Ops:
  0.0 205.3 %copy-start = (f32[1,16384]{1,0:T(1,128)S(1)}, f32[1,16384]{1,0:T(1,128)}, u32[]{:S(2)}) copy-start(f32[1,16384]{1,0:T(1,128)} %param.10) | copy-start | bytes 196612
  3.0 20.8 %all-to-all-start.2 = ((f32[8,2,128,128]{3,1,0,2:T(2,128)}), f32[8,2,128,128]{3,1,0,2:T(2,128)S(1)}, u32[]{:S(2)}, u32[]{:S(2)}) async-start(f32[8,2,128,128]{3,1,0,2:T(2,128)} %copy.26), calls=%async_computation.2 | async-start | bytes 2097152 | tf_op jit(solution)/shard_map/all_to_all | solution.py:45
  26.0 17.4 %collective-permute-start = (f32[64,2,16,128]{3,0,2,1:T(8,128)S(1)}, f32[64,2,16,128]{3,0,2,1:T(8,128)S(1)}, u32[]{:S(2)}, u32[]{:S(2)}) collective-permute-start(f32[64,2,16,128]{3,0,2,1:T(8,128)S(1)} %fusion), channel_id=1, source_target_pairs={{0,1},{1,2},{2,3},{3,4},{4,5},{5,6},{6,7},{7,8},{8,9},{9,10},{10,1... | collective-permute-start | bytes 3145736 | tf_op jit(solution)/shard_map/ppermute | solution.py:24
  28.9 0.7 copy-start.5
  30.8 0.7 copy-start.4
  43.7 25.3 %collective-permute-start.1 = (f32[64,2,16,128]{3,0,2,1:T(8,128)S(1)}, f32[64,2,16,128]{3,0,2,1:T(8,128)S(1)}, u32[]{:S(2)}, u32[]{:S(2)}) collective-permute-start(f32[64,2,16,128]{3,0,2,1:T(8,128)S(1)} %broadcast_select_fusion), channel_id=1, source_target_pairs={{0,2},{1,3},{2,4},{3,5},{4,6},{5,7},{6,8},{7,9},{8,10},{9,11},{10,... | collective-permute-start | bytes 3145736 | tf_op jit(solution)/shard_map/ppermute | solution.py:24
  69.2 23.6 %collective-permute-start.2 = (f32[64,2,16,128]{3,0,2,1:T(8,128)S(1)}, f32[64,2,16,128]{3,0,2,1:T(8,128)S(1)}, u32[]{:S(2)}, u32[]{:S(2)}) collective-permute-start(f32[64,2,16,128]{3,0,2,1:T(8,128)S(1)} %broadcast_select_fusion.1), channel_id=1, source_target_pairs={{0,4},{1,5},{2,6},{3,7},{4,8},{5,9},{6,10},{7,11},{8,12},{9,13},{1... | collective-permute-start | bytes 3145736 | tf_op jit(solution)/shard_map/ppermute | solution.py:24
  93.0 31.3 %collective-permute-start.3 = (f32[64,2,16,128]{3,0,2,1:T(8,128)S(1)}, f32[64,2,16,128]{3,0,2,1:T(8,128)S(1)}, u32[]{:S(2)}, u32[]{:S(2)}) collective-permute-start(f32[64,2,16,128]{3,0,2,1:T(8,128)S(1)} %broadcast_select_fusion.2), channel_id=1, source_target_pairs={{0,8},{1,9},{2,10},{3,11},{4,12},{5,13},{6,14},{7,15},{8,16},{9,17... | collective-permute-start | bytes 3145736 | tf_op jit(solution)/shard_map/ppermute | solution.py:24
  124.2 5.9 %copy-start.3 = (s32[8,2]{0,1:T(2,128)S(1)}, s32[8,2]{0,1:T(2,128)}, u32[]{:S(2)}) copy-start(s32[8,2]{0,1:T(2,128)} %param.9) | copy-start | bytes 196
  124.2 15.2 %copy-start.2 = (f32[8,2,1,16384]{3,2,1,0:T(1,128)S(1)}, f32[8,2,1,16384]{3,2,1,0:T(1,128)}, u32[]{:S(2)}) copy-start(f32[8,2,1,16384]{3,2,1,0:T(1,128)} %param.7) | copy-start | bytes 3145732
  124.5 50.0 %collective-permute-start.4 = (f32[64,2,16,128]{3,0,2,1:T(8,128)S(1)}, f32[64,2,16,128]{3,0,2,1:T(8,128)}, u32[]{:S(2)}, u32[]{:S(2)}) collective-permute-start(f32[64,2,16,128]{3,0,2,1:T(8,128)S(1)} %broadcast_select_fusion.3), channel_id=1, source_target_pairs={{0,16},{1,17},{2,18},{3,19},{4,20},{5,21},{6,22},{7,23},{8,24},{9,... | collective-permute-start | bytes 3145736 | tf_op jit(solution)/shard_map/ppermute | solution.py:24
  130.8 15.2 %all-to-all-start.1 = ((s32[8,8,2]{1,2,0:T(2,128)}), s32[8,8,2]{1,2,0:T(2,128)S(1)}, u32[]{:S(2)}, u32[]{:S(2)}) async-start(s32[8,8,2]{1,2,0:T(2,128)} %stack.2), calls=%async_computation.1 | async-start | bytes 16384 | tf_op jit(solution)/shard_map/all_to_all | solution.py:14
  146.0 59.5 %all-to-all-start = ((f32[8,2,128,128]{3,1,0,2:T(2,128)}), f32[8,2,128,128]{3,1,0,2:T(2,128)S(1)}, u32[]{:S(2)}, u32[]{:S(2)}) async-start(f32[8,2,128,128]{3,1,0,2:T(2,128)} %copy.22), calls=%async_computation | async-start | bytes 2097152 | tf_op jit(solution)/shard_map/all_to_all | solution.py:52
  175.9 52.4 %collective-permute-start.6 = (f32[64,2,16,128]{3,0,2,1:T(8,128)S(1)}, f32[64,2,16,128]{3,0,2,1:T(8,128)S(1)}, u32[]{:S(2)}, u32[]{:S(2)}) collective-permute-start(f32[64,2,16,128]{3,0,2,1:T(8,128)S(1)} %broadcast_select_fusion.4), channel_id=1, source_target_pairs={{0,1},{1,2},{2,3},{3,4},{4,5},{5,6},{6,7},{7,8},{8,9},{9,10},{10,1... | collective-permute-start | bytes 3145736 | tf_op jit(solution)/shard_map/ppermute | solution.py:24
  205.3 23.0 %collective-permute-start.5 = (f32[64,2,16,128]{3,0,2,1:T(8,128)S(1)}, f32[64,2,16,128]{3,0,2,1:T(8,128)}, u32[]{:S(2)}, u32[]{:S(2)}) collective-permute-start(f32[64,2,16,128]{3,0,2,1:T(8,128)S(1)} %broadcast_select_fusion.4), channel_id=1, source_target_pairs={{0,31},{1,0},{2,1},{3,2},{4,3},{5,4},{6,5},{7,6},{8,7},{9,8},{10,9... | collective-permute-start | bytes 3145736 | tf_op jit(solution)/shard_map/ppermute | solution.py:24
  285.7 1.2 copy-start.1
